TPU v7x, 128 devices: a whole 4x4x4 slice. The times are simulated.
128 devices in a mesh: rows: 16 (over z, x), sub: 8 (over y, core).
Axes of the slice: x: 4, y: 4, z: 4, core: 2. Of those that a mesh axis runs over, the one named last changes fastest.
Arguments:
- residuals: bfloat16 [65536, 1024], P(('rows', 'sub')), may hold values from -14 to 14
- codes: int32 [65536, 64], P(('rows', 'sub')), may hold values from 0 to 255, as said below
- codebook: bfloat16 [64, 16, 256], replicated, may hold values from -4 to 4
Outputs:
- rotated: bfloat16 [65536, 1024], P(('rows', 'sub'))
- new_codebook: float32 [64, 16, 256], P('sub', None, 'rows')
Inputs may be any that keep to these rules, and one draw needn't show every extreme that they name: `codes`: every codeword 0 to 255 occurs in every column.
All inputs are finite; a program needn't handle non-finite values.
Results may differ from a plain program's by a relative error of at most 0.0042.
Values may be sent and summed in bfloat16 or wider, within the bound.
A program may use at most 64 MiB of HBM per device.

v0:
```python
import jax
import jax.numpy as jnp
from jax import lax
from jax.sharding import PartitionSpec as P

D = 1024
SUBS = 64
CODES = 256
ITERS = 2


def rebuild(labels, codebook):
    rows = labels.shape[0]
    block = min(rows, 16384 // SUBS)
    levels = jnp.arange(CODES).astype(jnp.bfloat16)

    def one_block(piece):
        hot = (piece[:, :, None] == levels[None, None, :]).astype(jnp.bfloat16)
        rec = jnp.einsum("rmk,mdk->rmd", hot, codebook, preferred_element_type=jnp.float32)
        return rec.astype(jnp.bfloat16).reshape(block, D)

    return lax.map(one_block, labels.reshape(rows // block, block, SUBS)).reshape(rows, D)


def tally(values, labels, count):
    rows = values.shape[0]
    width = values.shape[1] // count
    block = min(rows, 16384 // count)
    levels = jnp.arange(CODES).astype(jnp.bfloat16)

    def one_step(index, carry):
        sums, totals = carry
        vals = lax.dynamic_slice_in_dim(values, index * block, block, 0).reshape(
            block, count, width
        )
        labs = lax.dynamic_slice_in_dim(labels, index * block, block, 0)
        hot = (labs[:, :, None] == levels[None, None, :]).astype(jnp.bfloat16)
        sums = sums + jnp.einsum("rmd,rmk->mdk", vals, hot, preferred_element_type=jnp.float32)
        totals = totals + jnp.sum(hot, axis=0, dtype=jnp.float32)
        return (sums, totals)

    start = (jnp.zeros((count, width, CODES), jnp.float32), jnp.zeros((count, CODES), jnp.float32))
    return lax.fori_loop(0, rows // block, one_step, start)


def iterate(polar, gram, make_gram):
    highest = lax.Precision.HIGHEST
    scale = jnp.sqrt(jnp.sqrt(jnp.sum(gram * gram) + 1e-06))
    polar = polar / scale
    gram = gram / (scale * scale)
    for step in range(ITERS):
        if step > 0:
            gram = make_gram(polar)
        moved = jnp.dot(polar, gram, precision=highest)
        polar = 3.4445 * polar - 4.775 * moved + 2.0315 * jnp.dot(moved, gram, precision=highest)
    return polar


def per_device(residuals, codes, codebook):
    labels = codes.astype(jnp.bfloat16)
    recon = rebuild(labels, codebook)
    highest = lax.Precision.HIGHEST
    contract = (((0,), (0,)), ((), ()))
    local = lax.dot_general(residuals, recon, contract, preferred_element_type=jnp.float32)
    cross = lax.psum(local, ("rows", "sub"))
    polar = cross / jnp.sqrt(jnp.sum(cross * cross) + 1e-06)

    def local_gram(current):
        return lax.dot_general(current, current, contract, precision=highest)

    polar = iterate(polar, local_gram(polar), local_gram)
    rotation = polar.astype(jnp.bfloat16)
    rotated = jnp.dot(residuals, rotation, preferred_element_type=jnp.float32).astype(jnp.bfloat16)
    owned_rows, owned_labels = (
        lax.all_to_all(rotated, "sub", split_axis=1, concat_axis=0, tiled=True),
        lax.all_to_all(labels, "sub", split_axis=1, concat_axis=0, tiled=True),
    )
    sums, totals = tally(owned_rows, owned_labels, owned_labels.shape[1])
    sums, totals = (
        lax.psum_scatter(sums, "rows", scatter_dimension=2, tiled=True),
        lax.psum_scatter(totals[:, None, :], "rows", scatter_dimension=2, tiled=True),
    )
    return (rotated, sums / totals)


def solution(mesh):
    return jax.shard_map(
        per_device,
        mesh=mesh,
        in_specs=(P(("rows", "sub"), None), P(("rows", "sub"), None), P()),
        out_specs=(P(("rows", "sub"), None), P("sub", None, "rows")),
        check_vma=False,
    )
```

profile of v0, /device:TPU:0, one launch (start us, length us, event | category | flops | bytes accessed | tf_op | source)
XLA Modules:
  0.0 439.1 jit_solution(3394257541561877917)
XLA Ops:
  8.2 8.8 %while.27 = (s32[]{:T(128)}, bf16[2,256,1024]{2,1,0:T(8,128)(2,1)S(1)}, bf16[2,256,64]{1,2,0:T(8,128)(2,1)S(1)}, bf16[64,16,256]{2,1,0:T(8,128)(2,1)}, s32[]{:T(128)}) while((s32[]{:T(128)}, bf16[2,256,1024]{2,1,0:T(8,128)(2,1)S(1)}, bf16[2,256,64]{1,2,0:T(8,128)(2,1)S(1)}, bf16[64,16,256]{2,1,0:T(8,128)(2,1)}, s32[]{:T(128)}) %tuple.70), condition=%wide.region_1.2_spmd.clone, body=%wide.region_0.1_spmd.clone.sunk | while | flops 138674432 | bytes 3245125 | solution.py:22
  8.3 4.1 fusion.45
  12.7 4.1 fusion.45
  17.1 3.3 convolution_bitcast_fusion
  20.3 156.7 %all-reduce.5.cloned.1.call-done = f32[1024,1024]{0,1:T(8,128)} async-done(((f32[1024,1024]{0,1:T(8,128)}), f32[1024,1024]{0,1:T(8,128)}) %all-reduce.5.cloned.1.call-update) | async-done | bytes 4194320 | tf_op jit(solution)/shard_map/psum | solution.py:65
  177.0 3.9 multiply_reduce_fusion.1
  181.6 19.1 %multiply_reduce_fusion = (f32[]{:T(128)}, f32[1024,1024]{1,0:T(8,128)}) fusion(f32[1024,1024]{0,1:T(8,128)} %all-reduce.5.cloned.1.call-done, f32[]{:T(128)S(6)} %sqrt.9), kind=kOutput, calls=%fused_computation.23 | convolution fusion | flops 12888047616 | bytes 8388616 | tf_op jit(solution)/shard_map/dot_general | solution.py:69
  201.4 18.0 %fusion.21 = f32[1024,1024]{1,0:T(8,128)} fusion(f32[1024,1024]{0,1:T(8,128)} %all-reduce.5.cloned.1.call-done, f32[]{:T(128)S(6)} %multiply.8, f32[1024,1024]{1,0:T(8,128)} %get-tuple-element.205, f32[]{:T(128)S(6)} %mul.38), kind=kOutput, calls=%fused_computation.31 | convolution fusion | flops 12886999040 | bytes 12582920 | tf_op jit(solution)/shard_map/dot_general | solution.py:54
  219.4 5.4 %copy.19 = f32[1024,1024]{0,1:T(8,128)} copy(f32[1024,1024]{1,0:T(8,128)} %fusion.21) | data formatting | bytes 8388608 | tf_op jit(solution)/shard_map/dot_general | solution.py:54
  224.7 27.6 %multiply_add_fusion = f32[1024,1024]{0,1:T(8,128)S(1)} fusion(f32[1024,1024]{0,1:T(8,128)} %copy.19, f32[1024,1024]{1,0:T(8,128)} %fusion.21, f32[1024,1024]{0,1:T(8,128)} %all-reduce.5.cloned.1.call-done, f32[]{:T(128)S(6)} %multiply.8, f32[1024,1024]{1,0:T(8,128)} %get-tuple-element.205, f32[]{:T(128)S(6)} %mul.38), kind=kOutput, calls=%fused_computation.22 | convolution fusion | flops 12892241920 | bytes 20971528 | tf_op jit(solution)/shard_map/dot_general | solution.py:55
  252.3 13.7 %fusion.22 = f32[1024,1024]{1,0:T(8,128)S(1)} fusion(f32[1024,1024]{0,1:T(8,128)S(1)} %multiply_add_fusion), kind=kOutput, calls=%fused_computation.36 | convolution fusion | flops 12884901888 | bytes 8388608 | tf_op jit(solution)/shard_map/dot_general | solution.py:69
  268.0 14.7 %fusion.23 = f32[1024,1024]{1,0:T(8,128)} fusion(f32[1024,1024]{0,1:T(8,128)S(1)} %multiply_add_fusion, f32[1024,1024]{1,0:T(8,128)S(1)} %fusion.22), kind=kOutput, calls=%fused_computation.37 | convolution fusion | flops 12884901888 | bytes 12582912 | tf_op jit(solution)/shard_map/dot_general | solution.py:54
  282.7 5.4 %copy.21 = f32[1024,1024]{0,1:T(8,128)} copy(f32[1024,1024]{1,0:T(8,128)} %fusion.23) | data formatting | bytes 8388608 | tf_op jit(solution)/shard_map/dot_general | solution.py:54
  288.1 19.3 %add_convert_fusion = bf16[1024,1024]{0,1:T(8,128)(2,1)S(1)} fusion(f32[1024,1024]{0,1:T(8,128)} %copy.21, f32[1024,1024]{0,1:T(8,128)} %copy-done.1, f32[1024,1024]{1,0:T(8,128)} %fusion.23, f32[1024,1024]{1,0:T(8,128)} %copy-done.2), kind=kOutput, calls=%fused_computation.21 | convolution fusion | flops 12891193344 | bytes 18874368 | tf_op jit(solution)/shard_map/dot_general | solution.py:55
  309.6 4.4 all-to-all-start
  314.6 15.3 %all-to-all-done = bf16[512,8,128]{0,2,1:T(8,128)(2,1)S(1)} async-done(((bf16[512,8,128]{0,2,1:T(8,128)(2,1)}), bf16[512,8,128]{0,2,1:T(8,128)(2,1)S(1)}, u32[]{:S(2)}, u32[]{:S(2)}) %all-to-all-start) | async-done | bytes 1048608 | tf_op jit(solution)/shard_map/all_to_all | solution.py:75
  330.0 3.4 all-to-all-start.1
  333.5 5.4 %all-to-all-done.1 = bf16[512,8,8]{0,2,1:T(8,128)(2,1)S(1)} async-done(((bf16[512,8,8]{0,2,1:T(8,128)(2,1)}), bf16[512,8,8]{0,2,1:T(8,128)(2,1)S(1)}, u32[]{:S(2)}, u32[]{:S(2)}) %all-to-all-start.1) | async-done | bytes 65568 | tf_op jit(solution)/shard_map/all_to_all | solution.py:76
  338.9 11.1 %while.28 = (s32[]{:T(128)}, f32[8,16,256]{2,1,0:T(8,128)S(1)}, f32[8,256]{1,0:T(8,128)S(1)}, bf16[4096,128]{0,1:T(8,128)(2,1)S(1)}, bf16[4096,8]{0,1:T(8,128)(2...) while((s32[]{:T(128)}, f32[8,16,256]{2,1,0:T(8,128)S(1)}, f32[8,256]{1,0:T(8,128)S(1)}, ...), condition=%wide.region_7.8_spmd.clone, body=%wide.region_5.7_spmd.clone.sunk | while | flops 155257088 | bytes 2000542 | solution.py:43
  338.9 2.9 fusion.48
  341.9 2.5 convert_reduce_fusion.2
  344.5 2.9 fusion.48
  354.2 39.1 %all-reduce.1 = f32[8,1,256]{2,0,1:T(8,128)S(1)} all-reduce(f32[8,1,256]{2,0,1:T(8,128)S(1)} %bitcast.64), channel_id=3, replica_groups=mesh['rows'=16,'sub'=8] {'rows'}, use_global_device_ids=true, to_apply=%region_9.10.clone | all-reduce | flops 2048 | bytes 16384
  393.4 36.8 %all-reduce.7.cloned.1.call-done = f32[8,16,256]{2,1,0:T(8,128)} async-done(((f32[8,16,256]{2,1,0:T(8,128)}), f32[8,16,256]{2,1,0:T(8,128)}) %all-reduce.7.cloned.1.call-update) | async-done | bytes 131088
  (45 shorter events, 14.4 us)
Async XLA Ops:
  7.2 9.9 %copy-start = (bf16[512,1024]{1,0:T(8,128)(2,1)S(1)}, bf16[512,1024]{1,0:T(8,128)(2,1)}, u32[]{:S(2)}) copy-start(bf16[512,1024]{1,0:T(8,128)(2,1)} %param.7) | copy-start | bytes 3145732
  7.2 169.9 %all-reduce.5.cloned.1.call-start = ((), (), s32[]{:S(2)}) async-start(), calls=%async_computation.2 | async-start | bytes 8388608 | tf_op jit(solution)/shard_map/psum | solution.py:65
  252.3 13.7 %copy-start.1 = (f32[1024,1024]{0,1:T(8,128)}, f32[1024,1024]{0,1:T(8,128)S(1)}, u32[]{:S(2)}) copy-start(f32[1024,1024]{0,1:T(8,128)S(1)} %multiply_add_fusion) | copy-start | bytes 12582916
  266.0 1.9 copy-start.2
  307.4 6.6 %copy-start.3 = (s32[512,64]{0,1:T(8,128)S(1)}, s32[512,64]{0,1:T(8,128)}, u32[]{:S(2)}) copy-start(s32[512,64]{0,1:T(8,128)} %param.8) | copy-start | bytes 393220
  309.6 20.3 %all-to-all-start = ((bf16[512,8,128]{0,2,1:T(8,128)(2,1)}), bf16[512,8,128]{0,2,1:T(8,128)(2,1)S(1)}, u32[]{:S(2)}, u32[]{:S(2)}) async-start(bf16[512,8,128]{0,2,1:T(8,128)(2,1)} %bitcast.3), calls=%async_computation | async-start | bytes 2097152 | tf_op jit(solution)/shard_map/all_to_all | solution.py:75
  330.0 8.9 %all-to-all-start.1 = ((bf16[512,8,8]{0,2,1:T(8,128)(2,1)}), bf16[512,8,8]{0,2,1:T(8,128)(2,1)S(1)}, u32[]{:S(2)}, u32[]{:S(2)}) async-start(bf16[512,8,8]{0,2,1:T(8,128)(2,1)} %convert_bitcast_fusion), calls=%async_computation.1 | async-start | bytes 131072 | tf_op jit(solution)/shard_map/all_to_all | solution.py:76
  333.3 97.0 %all-reduce.7.cloned.1.call-start = ((), (), s32[]{:S(2)}) async-start(), calls=%async_computation.3 | async-start | bytes 262144
  338.9 11.8 %copy-start.5 = (u32[128]{0:T(128)S(1)}, u32[128]{0:T(128)}, u32[]{:S(2)}) copy-start(u32[128]{0:T(128)} %constant.61) | copy-start | bytes 1540
  350.0 0.7 copy-start.4
Sparse Core Ops, SparseCore 0:
  20.5 156.5 all-reduce.4
  350.8 79.4 all-reduce.6
where the time goes:
time: 448 us; the launch traced here: 439 us
  waiting for transfers between devices  214 us (48%)
  matrix products  132 us (29%)
  blocking collectives  39.1 us (9%)
  local copies, waits for them, and re-layouts  17 us (4%)
  between operations  16.7 us (4%)
  other arithmetic  12.1 us (3%)
  starting transfers between devices  7.78 us (2%)
    psum x1, waiting for transfers between devices, per_device(): cross = lax.psum(local, ('rows', 'sub'))  157 us
    dot_general x2, matrix products, iterate(): jnp.dot(moved, gram, precision=highest)  46.9 us
    unnamed x1, blocking collectives  39.1 us
    unnamed x3, waiting for transfers between devices  36.9 us
    dot_general x2, matrix products, local_gram(): return lax.dot_general(current, current, contract, precision=highest)  32.8 us
    dot_general x2, matrix products, iterate(): moved = jnp.dot(polar, gram, precision=highest)  32.7 us
    all_to_all x1, waiting for transfers between devices, per_device(): lax.all_to_all(rotated, 'sub', split_axis=1, concat_axis=0, tiled=True)  15.3 us
    dot_general x2, local copies, waits for them, and re-layouts, iterate(): moved = jnp.dot(polar, gram, precision=highest)  10.7 us
  transfers between devices with their start and end apart: 4, of which 4 were waited for; matrix products, arithmetic and copies ran while one was open for 1% of the time, Pallas kernels for 0%

commit v1 on v0

--- a/solution.py
+++ b/solution.py
@@ -7,6 +7,10 @@
 SUBS = 64
 CODES = 256
 ITERS = 2
+
+
+def _start_plane(u_in, mesh_ax, along_axis):
+    return jax.lax.psum(jax.lax.psum(u_in, axis_name=mesh_ax), axis_name=along_axis)
 
 
 def rebuild(labels, codebook):
@@ -62,7 +66,7 @@
     highest = lax.Precision.HIGHEST
     contract = (((0,), (0,)), ((), ()))
     local = lax.dot_general(residuals, recon, contract, preferred_element_type=jnp.float32)
-    cross = lax.psum(local, ("rows", "sub"))
+    cross = _start_plane(local, "rows", "sub")
     polar = cross / jnp.sqrt(jnp.sum(cross * cross) + 1e-06)
 
     def local_gram(current):

time: 448 us -> 473 us (1.056)
  waiting for transfers between devices: 214 us -> 239 us
    psum x1 -> x2, waiting for transfers between devices: 157 us -> 181 us  [the longest x1 106 us: _start_plane(): jax.lax.psum(u_in, axis_name=mesh_ax)]
    unnamed x3 -> x4, waiting for transfers between devices: 36.9 us -> 37.3 us
  transfers between devices with their start and end apart: 4 -> 5, of which waited for: 4 -> 5; matrix products, arithmetic and copies ran while one was open for 1% -> 1% of each run, Pallas kernels for 0% -> 0%
where the time goes in v1:
time: 473 us; the launch traced here: 464 us
  waiting for transfers between devices  239 us (51%)
  matrix products  132 us (28%)
  blocking collectives  41 us (9%)
  local copies, waits for them, and re-layouts  17 us (4%)
  between operations  16.5 us (3%)
  other arithmetic  12.1 us (3%)
  starting transfers between devices  7.03 us (1%)
    psum x1, waiting for transfers between devices, _start_plane(): jax.lax.psum(u_in, axis_name=mesh_ax)  106 us
    psum x1, waiting for transfers between devices, _start_plane(): jax.lax.psum(jax.lax.psum(u_in, axis_name=mesh_ax), axis_name=along_axis)  74.6 us
    dot_general x2, matrix products, iterate(): jnp.dot(moved, gram, precision=highest)  46.9 us
    unnamed x1, blocking collectives  41 us
    unnamed x4, waiting for transfers between devices  37.3 us
    dot_general x2, matrix products, local_gram(): return lax.dot_general(current, current, contract, precision=highest)  32.8 us
    dot_general x2, matrix products, iterate(): moved = jnp.dot(polar, gram, precision=highest)  32.7 us
    all_to_all x1, waiting for transfers between devices, per_device(): lax.all_to_all(rotated, 'sub', split_axis=1, concat_axis=0, tiled=True)  15.2 us
  transfers between devices with their start and end apart: 5, of which 5 were waited for; matrix products, arithmetic and copies ran while one was open for 1% of the time, Pallas kernels for 0%

profile of v1, /device:TPU:0, one launch (start us, length us, event | category | flops | bytes accessed | tf_op | source)
XLA Modules:
  0.0 464.4 jit_solution(6452656530811824396)
XLA Ops:
  8.2 8.8 %while.27 = (s32[]{:T(128)}, bf16[2,256,1024]{2,1,0:T(8,128)(2,1)S(1)}, bf16[2,256,64]{1,2,0:T(8,128)(2,1)S(1)}, bf16[64,16,256]{2,1,0:T(8,128)(2,1)}, s32[]{:T(128)}) while((s32[]{:T(128)}, bf16[2,256,1024]{2,1,0:T(8,128)(2,1)S(1)}, bf16[2,256,64]{1,2,0:T(8,128)(2,1)S(1)}, bf16[64,16,256]{2,1,0:T(8,128)(2,1)}, s32[]{:T(128)}) %tuple.72), condition=%wide.region_1.2_spmd.clone, body=%wide.region_0.1_spmd.clone.sunk | while | flops 138674432 | bytes 3245125 | solution.py:26
  8.3 4.1 fusion.45
  12.7 4.1 fusion.45
  17.1 3.2 convolution_bitcast_fusion
  20.4 106.2 %all-reduce.6.cloned.1.call-done = f32[1024,1024]{0,1:T(8,128)} async-done(((f32[1024,1024]{0,1:T(8,128)}), f32[1024,1024]{0,1:T(8,128)}) %all-reduce.6.cloned.1.call-update) | async-done | bytes 4194320 | tf_op jit(solution)/shard_map/psum | solution.py:13
  126.6 74.6 %all-reduce.8.cloned.1.call-done = f32[1024,1024]{0,1:T(8,128)} async-done(((f32[1024,1024]{0,1:T(8,128)}), f32[1024,1024]{0,1:T(8,128)}) %all-reduce.8.cloned.1.call-update) | async-done | bytes 4194320 | tf_op jit(solution)/shard_map/psum | solution.py:13
  201.2 3.9 multiply_reduce_fusion.1
  205.8 19.1 %multiply_reduce_fusion = (f32[]{:T(128)}, f32[1024,1024]{1,0:T(8,128)}) fusion(f32[1024,1024]{0,1:T(8,128)} %all-reduce.8.cloned.1.call-done, f32[]{:T(128)S(6)} %sqrt.9), kind=kOutput, calls=%fused_computation.23 | convolution fusion | flops 12888047616 | bytes 8388616 | tf_op jit(solution)/shard_map/dot_general | solution.py:73
  225.6 18.0 %fusion.21 = f32[1024,1024]{1,0:T(8,128)} fusion(f32[1024,1024]{0,1:T(8,128)} %all-reduce.8.cloned.1.call-done, f32[]{:T(128)S(6)} %multiply.8, f32[1024,1024]{1,0:T(8,128)} %get-tuple-element.205, f32[]{:T(128)S(6)} %mul.38), kind=kOutput, calls=%fused_computation.31 | convolution fusion | flops 12886999040 | bytes 12582920 | tf_op jit(solution)/shard_map/dot_general | solution.py:58
  243.5 5.4 %copy.19 = f32[1024,1024]{0,1:T(8,128)} copy(f32[1024,1024]{1,0:T(8,128)} %fusion.21) | data formatting | bytes 8388608 | tf_op jit(solution)/shard_map/dot_general | solution.py:58
  248.9 27.6 %multiply_add_fusion = f32[1024,1024]{0,1:T(8,128)S(1)} fusion(f32[1024,1024]{0,1:T(8,128)} %copy.19, f32[1024,1024]{1,0:T(8,128)} %fusion.21, f32[1024,1024]{0,1:T(8,128)} %all-reduce.8.cloned.1.call-done, f32[]{:T(128)S(6)} %multiply.8, f32[1024,1024]{1,0:T(8,128)} %get-tuple-element.205, f32[]{:T(128)S(6)} %mul.38), kind=kOutput, calls=%fused_computation.22 | convolution fusion | flops 12892241920 | bytes 20971528 | tf_op jit(solution)/shard_map/dot_general | solution.py:59
  276.5 13.7 %fusion.22 = f32[1024,1024]{1,0:T(8,128)S(1)} fusion(f32[1024,1024]{0,1:T(8,128)S(1)} %multiply_add_fusion), kind=kOutput, calls=%fused_computation.36 | convolution fusion | flops 12884901888 | bytes 8388608 | tf_op jit(solution)/shard_map/dot_general | solution.py:73
  292.1 14.7 %fusion.23 = f32[1024,1024]{1,0:T(8,128)} fusion(f32[1024,1024]{0,1:T(8,128)S(1)} %multiply_add_fusion, f32[1024,1024]{1,0:T(8,128)S(1)} %fusion.22), kind=kOutput, calls=%fused_computation.37 | convolution fusion | flops 12884901888 | bytes 12582912 | tf_op jit(solution)/shard_map/dot_general | solution.py:58
  306.9 5.4 %copy.21 = f32[1024,1024]{0,1:T(8,128)} copy(f32[1024,1024]{1,0:T(8,128)} %fusion.23) | data formatting | bytes 8388608 | tf_op jit(solution)/shard_map/dot_general | solution.py:58
  312.2 19.3 %add_convert_fusion = bf16[1024,1024]{0,1:T(8,128)(2,1)S(1)} fusion(f32[1024,1024]{0,1:T(8,128)} %copy.21, f32[1024,1024]{0,1:T(8,128)} %copy-done.1, f32[1024,1024]{1,0:T(8,128)} %fusion.23, f32[1024,1024]{1,0:T(8,128)} %copy-done.2), kind=kOutput, calls=%fused_computation.21 | convolution fusion | flops 12891193344 | bytes 18874368 | tf_op jit(solution)/shard_map/dot_general | solution.py:59
  333.8 3.6 all-to-all-start
  338.0 15.2 %all-to-all-done = bf16[512,8,128]{0,2,1:T(8,128)(2,1)S(1)} async-done(((bf16[512,8,128]{0,2,1:T(8,128)(2,1)}), bf16[512,8,128]{0,2,1:T(8,128)(2,1)S(1)}, u32[]{:S(2)}, u32[]{:S(2)}) %all-to-all-start) | async-done | bytes 1048608 | tf_op jit(solution)/shard_map/all_to_all | solution.py:79
  353.3 3.4 all-to-all-start.1
  356.8 5.4 %all-to-all-done.1 = bf16[512,8,8]{0,2,1:T(8,128)(2,1)S(1)} async-done(((bf16[512,8,8]{0,2,1:T(8,128)(2,1)}), bf16[512,8,8]{0,2,1:T(8,128)(2,1)S(1)}, u32[]{:S(2)}, u32[]{:S(2)}) %all-to-all-start.1) | async-done | bytes 65568 | tf_op jit(solution)/shard_map/all_to_all | solution.py:80
  362.2 11.1 %while.28 = (s32[]{:T(128)}, f32[8,16,256]{2,1,0:T(8,128)S(1)}, f32[8,256]{1,0:T(8,128)S(1)}, bf16[4096,128]{0,1:T(8,128)(2,1)S(1)}, bf16[4096,8]{0,1:T(8,128)(2...) while((s32[]{:T(128)}, f32[8,16,256]{2,1,0:T(8,128)S(1)}, f32[8,256]{1,0:T(8,128)S(1)}, ...), condition=%wide.region_8.9_spmd.clone, body=%wide.region_6.8_spmd.clone.sunk | while | flops 155257088 | bytes 2000542 | solution.py:47
  362.2 2.9 fusion.48
  367.8 2.9 fusion.48
  377.5 41.0 %all-reduce.1 = f32[8,1,256]{2,0,1:T(8,128)S(1)} all-reduce(f32[8,1,256]{2,0,1:T(8,128)S(1)} %bitcast.64), channel_id=3, replica_groups=mesh['rows'=16,'sub'=8] {'rows'}, use_global_device_ids=true, to_apply=%region_10.11.clone | all-reduce | flops 2048 | bytes 16384
  418.6 37.3 %all-reduce.10.cloned.1.call-done = f32[8,16,256]{2,1,0:T(8,128)} async-done(((f32[8,16,256]{2,1,0:T(8,128)}), f32[8,16,256]{2,1,0:T(8,128)}) %all-reduce.10.cloned.1.call-update) | async-done | bytes 131088
  (48 shorter events, 17.0 us)
Async XLA Ops:
  7.2 9.9 %copy-start = (bf16[512,1024]{1,0:T(8,128)(2,1)S(1)}, bf16[512,1024]{1,0:T(8,128)(2,1)}, u32[]{:S(2)}) copy-start(bf16[512,1024]{1,0:T(8,128)(2,1)} %param.7) | copy-start | bytes 3145732
  7.2 119.4 %all-reduce.6.cloned.1.call-start = ((), (), s32[]{:S(2)}) async-start(), calls=%async_computation.2 | async-start | bytes 8388608 | tf_op jit(solution)/shard_map/psum | solution.py:13
  20.3 180.9 %all-reduce.8.cloned.1.call-start = ((), (), s32[]{:S(2)}) async-start(), calls=%async_computation.3 | async-start | bytes 8388608 | tf_op jit(solution)/shard_map/psum | solution.py:13
  276.5 13.7 %copy-start.1 = (f32[1024,1024]{0,1:T(8,128)}, f32[1024,1024]{0,1:T(8,128)S(1)}, u32[]{:S(2)}) copy-start(f32[1024,1024]{0,1:T(8,128)S(1)} %multiply_add_fusion) | copy-start | bytes 12582916
  290.2 1.9 copy-start.2
  331.5 5.8 %copy-start.3 = (s32[512,64]{0,1:T(8,128)S(1)}, s32[512,64]{0,1:T(8,128)}, u32[]{:S(2)}) copy-start(s32[512,64]{0,1:T(8,128)} %param.8) | copy-start | bytes 393220
  333.8 19.4 %all-to-all-start = ((bf16[512,8,128]{0,2,1:T(8,128)(2,1)}), bf16[512,8,128]{0,2,1:T(8,128)(2,1)S(1)}, u32[]{:S(2)}, u32[]{:S(2)}) async-start(bf16[512,8,128]{0,2,1:T(8,128)(2,1)} %bitcast.3), calls=%async_computation | async-start | bytes 2097152 | tf_op jit(solution)/shard_map/all_to_all | solution.py:79
  353.3 8.9 %all-to-all-start.1 = ((bf16[512,8,8]{0,2,1:T(8,128)(2,1)}), bf16[512,8,8]{0,2,1:T(8,128)(2,1)S(1)}, u32[]{:S(2)}, u32[]{:S(2)}) async-start(bf16[512,8,8]{0,2,1:T(8,128)(2,1)} %convert_bitcast_fusion), calls=%async_computation.1 | async-start | bytes 131072 | tf_op jit(solution)/shard_map/all_to_all | solution.py:80
  356.6 99.3 %all-reduce.10.cloned.1.call-start = ((), (), s32[]{:S(2)}) async-start(), calls=%async_computation.4 | async-start | bytes 262144
  362.2 11.8 %copy-start.5 = (u32[128]{0:T(128)S(1)}, u32[128]{0:T(128)}, u32[]{:S(2)}) copy-start(u32[128]{0:T(128)} %constant.61) | copy-start | bytes 1540
  373.3 0.7 copy-start.4
Sparse Core Ops, SparseCore 0:
  20.4 106.0 all-reduce.5
  128.9 72.2 all-reduce.7
  374.1 81.7 all-reduce.9
